TPU v7x, 512 devices: a whole 4x4x16 slice. The times are simulated.
512 devices in a mesh: dp: 4 (over x), cand: 32 (over z, core), tensor: 4 (over y).
Axes of the slice: x: 4, y: 4, z: 16, core: 2. Of those that a mesh axis runs over, the one named last changes fastest.
Arguments:
- context: bfloat16 [8, 4096, 3584], P('dp', 'cand', 'tensor'), may hold values from -12 to 12
- residual: bfloat16 [8, 4096, 3584], P('dp', ('cand', 'tensor')), may hold values from -36 to 36
- out_weight: bfloat16 [3584, 3584], P('cand', 'tensor'), may hold values from -0.09375 to 0.09375
- adapter_down: bfloat16 [3584, 16], P('tensor'), may hold values from -0.09375 to 0.09375
- adapter_up_weight: bfloat16 [16, 3584], replicated, may hold values from -1.5 to 1.5
- norm_gain: float32 [3584], replicated, may hold values from 0.5 to 1.5
- score_weight: float32 [3584], replicated, may hold values from -0.09375 to 0.09375
- teacher: bfloat16 [8, 4096, 4096], P('dp', 'cand', 'tensor'), may hold values from 0.019897461 to 0.9765625
- pair_mask: int32 [8, 4096, 4096], P('dp', 'cand', 'tensor'), may hold values from 0 to 1, as said below
- loss_scale: float32 [8], P('dp'), may hold values from 65536 to 262144
Outputs:
- context_grad: bfloat16 [8, 4096, 3584], P('dp', 'cand', 'tensor')
- residual_gradient: bfloat16 [8, 4096, 3584], P('dp', ('cand', 'tensor'))
- down_grad: float32 [3584, 16], P('tensor')
- up_weight_gradient: float32 [16, 3584], P(None, 'tensor')
- pair_loss: float32 [8], P('dp')
Inputs may be any that keep to these rules, and one draw needn't show every extreme that they name: pair_mask holds 0 or 1; with P = 32, every pair (i, j) whose group j // P lies 4096 / (2P) groups after i // P, counted round over the 4096 / P groups, is valid.
All inputs are finite; a program needn't handle non-finite values.
Results may differ from a plain program's by a relative error of at most 0.02.
Values may be sent and summed in bfloat16 or wider, within the bound.
No kernel may reach another device: no remote copies, remote signals or barrier semaphores. Data moves between devices by JAX's collectives and lax.ppermute only.
A program may use at most 64 MiB of HBM per device.

v0:
```python
import jax
import jax.numpy as jnp
from jax import lax
from jax.sharding import PartitionSpec as P

ADAPTER_SCALE = 0.5
epsilon = 1e-06


def rounded(term):
    return lax.optimization_barrier(term.astype(jnp.bfloat16)).astype(jnp.float32)


def pair_terms(all_scores, own_scores, teacher, valid_pairs, row_start, col_start):
    column_scores = lax.dynamic_slice_in_dim(all_scores, col_start, teacher.shape[2], 1)
    margin = own_scores[:, :, None] - column_scores[:, None, :]
    target = teacher.astype(jnp.float32)
    total = jnp.sum(valid_pairs * (jax.nn.softplus(margin) - target * margin), axis=(1, 2))
    slope = valid_pairs * (jax.nn.sigmoid(margin) - target)
    blank = jnp.zeros(all_scores.shape, jnp.float32)
    row_part = lax.dynamic_update_slice_in_dim(blank, jnp.sum(slope, axis=2), row_start, 1)
    column_part = lax.dynamic_update_slice_in_dim(blank, jnp.sum(slope, axis=1), col_start, 1)
    return (total, row_part - column_part)


def on_device(
    context,
    residual,
    out_weight,
    adapter_down,
    adapter_up_weight,
    norm_gain,
    score_weight,
    teacher,
    pair_mask,
    loss_scale,
):
    cand_rows = context.shape[1]
    tensor_count = lax.axis_size("tensor")
    share = cand_rows // tensor_count
    tensor_index = lax.axis_index("tensor")
    group_index = lax.axis_index("cand")
    valid_pairs = pair_mask.astype(jnp.float32)
    mask_count = jnp.sum(valid_pairs, axis=(1, 2))
    count = lax.psum(mask_count, ("cand", "tensor"))
    low_terms = rounded(
        jnp.einsum("qch,hr->qcr", context, adapter_down, preferred_element_type=jnp.float32)
    )
    full_weight = lax.all_gather(out_weight, "cand", axis=0, tiled=True)
    head_terms = jnp.einsum("qch,dh->qcd", context, full_weight, preferred_element_type=jnp.float32)
    head_terms = rounded(head_terms)
    summed_output, low_sum = (
        lax.psum_scatter(
            head_terms.astype(jnp.bfloat16), "tensor", scatter_dimension=1, tiled=True
        ).astype(jnp.float32),
        lax.psum_scatter(
            low_terms.astype(jnp.bfloat16), "tensor", scatter_dimension=1, tiled=True
        ).astype(jnp.float32),
    )
    adapter_input_rows = low_sum.astype(jnp.bfloat16)
    lifted_rows = jnp.einsum(
        "qcr,rd->qcd", adapter_input_rows, adapter_up_weight, preferred_element_type=jnp.float32
    )
    hidden_state = (
        residual.astype(jnp.float32) + summed_output + ADAPTER_SCALE * lifted_rows
    ).astype(jnp.bfloat16)
    hidden_wide = hidden_state.astype(jnp.float32)
    inv_rms = lax.rsqrt(jnp.mean(hidden_wide * hidden_wide, axis=2, keepdims=True) + epsilon)
    scores = jnp.sum(hidden_wide * inv_rms * norm_gain * score_weight, axis=2)
    all_scores = lax.all_gather(scores, ("cand", "tensor"), axis=1, tiled=True)
    own_start = group_index * cand_rows + tensor_index * share
    row_start = group_index * cand_rows
    col_start = tensor_index * teacher.shape[2]
    own_scores = lax.dynamic_slice_in_dim(all_scores, row_start, cand_rows, 1)
    total, score_vector = pair_terms(
        all_scores, own_scores, teacher, valid_pairs, row_start, col_start
    )
    summed_grad, loss_sum = lax.psum((score_vector, total), ("cand", "tensor"))
    pair_loss = loss_sum / count
    factor = loss_scale / count
    score_grad = lax.dynamic_slice_in_dim(summed_grad, own_start, share, 1) * factor[:, None]
    back_step = score_grad[:, :, None] * norm_gain * score_weight
    grad_hidden = inv_rms * back_step - hidden_wide * inv_rms**3 * jnp.mean(
        hidden_wide * back_step, axis=2, keepdims=True
    )
    grad_rows = grad_hidden.astype(jnp.bfloat16)
    adapter_rows = (
        ADAPTER_SCALE
        * jnp.einsum(
            "qcd,rd->qcr", grad_rows, adapter_up_weight, preferred_element_type=jnp.float32
        )
    ).astype(jnp.bfloat16)
    full_grads, full_adapter = (
        lax.all_gather(grad_rows, "tensor", axis=1, tiled=True),
        lax.all_gather(adapter_rows, "tensor", axis=1, tiled=True),
    )
    up_partial_gradient = ADAPTER_SCALE * jnp.einsum(
        "qcr,qcd->rd", adapter_input_rows, grad_rows, preferred_element_type=jnp.float32
    )
    up_share = lax.psum_scatter(
        up_partial_gradient.astype(jnp.bfloat16), "tensor", scatter_dimension=1, tiled=True
    ).astype(jnp.float32)
    adapter_back = jnp.einsum(
        "qcr,hr->qch", full_adapter, adapter_down, preferred_element_type=jnp.float32
    )
    context_wide = (
        jnp.einsum("qcd,dh->qch", full_grads, full_weight, preferred_element_type=jnp.float32)
        + adapter_back
    )
    context_grad = context_wide.astype(jnp.bfloat16)
    down_local = jnp.einsum(
        "qch,qcr->hr", context, full_adapter, preferred_element_type=jnp.float32
    )
    down_grad, up_weight_gradient = lax.psum((down_local, up_share), ("dp", "cand"))
    return (context_grad, grad_rows, down_grad, up_weight_gradient, pair_loss)


def solution(mesh):
    in_specs = (
        P("dp", "cand", "tensor"),
        P("dp", ("cand", "tensor"), None),
        P("cand", "tensor"),
        P("tensor", None),
        P(),
        P(),
        P(),
        P("dp", "cand", "tensor"),
        P("dp", "cand", "tensor"),
        P("dp"),
    )
    out_specs = (
        P("dp", "cand", "tensor"),
        P("dp", ("cand", "tensor"), None),
        P("tensor", None),
        P(None, "tensor"),
        P("dp"),
    )
    return jax.shard_map(
        on_device, mesh=mesh, in_specs=in_specs, out_specs=out_specs, check_vma=False
    )
```

profile of v0, /device:TPU:16, one launch (start us, length us, event | category | flops | bytes accessed | tf_op | source)
XLA Modules:
  0.0 1309.3 jit_solution(4041656282521602248)
XLA Ops:
  8.1 0.7 all-gather.4.cloned.1.call-update
  9.0 0.9 convolution_convert_fusion
  10.2 0.7 reshape.41
  11.0 81.7 %all-gather.4.cloned.1.call-done = bf16[3584,896]{1,0:T(8,128)(2,1)} async-done(((bf16[112,896]{1,0:T(8,128)(2,1)}), bf16[3584,896]{1,0:T(8,128)(2,1)}) %all-gather.4.cloned.1.call-update) | async-done | bytes 6422544 | tf_op jit(solution)/shard_map/all_gather | solution.py:49
  92.7 6.2 fusion.4
  99.0 0.8 reshape.42
  99.8 0.7 copy.21
  100.4 29.0 %reduce-scatter.8.cloned.1.call-done = bf16[2,32,3584]{2,1,0:T(8,128)(2,1)} async-done(((bf16[2,128,3584]{2,1,0:T(8,128)(2,1)}), bf16[2,32,3584]{2,1,0:T(8,128)(2,1)}) %reduce-scatter.8.cloned.1.call-update) | async-done | bytes 458768 | tf_op jit(solution)/shard_map/reduce_scatter | solution.py:53
  129.5 1.5 multiply_reduce_fusion.2
  131.0 0.3 multiply_reduce_fusion.1
  131.3 140.3 %all-gather = f32[128,32,2]{1,2,0:T(2,128)S(1)} all-gather(f32[1,32,2]{1,2,0:T(2,128)S(1)} %bitcast.57), channel_id=1, replica_groups=mesh['dp'=4,'cand'=32,'tensor'=4] {'cand','tensor'}, dimensions={0}, use_global_device_ids=true | all-gather | bytes 33024 | tf_op jit(solution)/shard_map/all_gather | solution.py:70
  271.8 1.2 fusion.24
  273.3 493.2 %all-reduce = (f32[2,4096]{1,0:T(2,128)S(1)}, f32[2]{0:T(128)S(1)}, f32[2]{0:T(128)S(1)}) all-reduce(f32[2,4096]{1,0:T(2,128)S(1)} %sub.29, f32[2]{0:T(128)S(1)} %get-tuple-element.6, f32[2]{0:T(128)S(1)} %get-tuple-element.5), channel_id=1, replica_groups=mesh['dp'=4,'cand'=32,'tensor'=4] {'cand','tensor'}, use_global_device_ids=true, to_apply=%region_6.7 | all-reduce | flops 8196 | bytes 65568 | tf_op jit(solution)/shard_map/psum | solution.py:78
  766.4 1.2 fusion.32
  767.7 0.3 multiply_reduce_fusion
  768.5 1.3 copy.22
  769.9 0.7 all-gather.6.cloned.1.call-update
  770.6 1.4 fusion.13
  772.1 13.7 %all_gather.15 = bf16[2,128,16]{2,0,1:T(2,128)(2,1)S(1)} all-gather(bf16[2,32,16]{2,0,1:T(2,128)(2,1)S(1)} %copy.17), channel_id=1, replica_groups=mesh['dp'=4,'cand'=32,'tensor'=4] {'tensor'}, dimensions={1}, use_global_device_ids=true | all-gather | bytes 10240 | tf_op jit(solution)/shard_map/all_gather | solution.py:95
  786.1 13.0 reduce-scatter.12.cloned.1.call-done
  799.1 1.0 copy.23
  800.1 495.1 %all-reduce.3 = (f32[896,16]{0,1:T(8,128)}, f32[16,896]{1,0:T(8,128)}) all-reduce(f32[896,16]{0,1:T(8,128)S(1)} %convolution_bitcast_fusion.1, bf16[16,896]{1,0:T(8,128)(2,1)S(1)} %copy.23), channel_id=1, replica_groups=mesh['dp'=4,'cand'=32,'tensor'=4] {'dp','cand'}, use_global_device_ids=true, to_apply=%region_10.11 | all-reduce | flops 28672 | bytes 200704 | tf_op jit(solution)/shard_map/psum | solution.py:114
  1295.2 5.5 fusion
  1300.6 1.1 fusion.12
  (49 shorter events, 2.1 us)
Async XLA Ops:
  8.0 1.0 copy-start
  8.0 84.7 %all-gather.4.cloned.1.call-start = ((), (), s32[]{:S(2)}) async-start(), calls=%async_computation.3 | async-start | bytes 6623232 | tf_op jit(solution)/shard_map/all_gather | solution.py:49
  8.7 90.2 %reduce-scatter.10.cloned.1.call-start = ((), (), s32[]{:S(2)}) async-start(), calls=%async_computation.6 | async-start | bytes 40960
  10.9 118.6 %copy-start.4 = (bf16[2,32,3584]{2,1,0:T(8,128)(2,1)S(1)}, bf16[2,32,3584]{2,1,0:T(8,128)(2,1)}, u32[]{:S(2)}) copy-start(bf16[2,32,3584]{2,1,0:T(8,128)(2,1)} %param.11) | copy-start | bytes 1376260
  10.9 118.6 %copy-start.5 = (bf16[16,3584]{1,0:T(8,128)(2,1)S(1)}, bf16[16,3584]{1,0:T(8,128)(2,1)}, u32[]{:S(2)}) copy-start(bf16[16,3584]{1,0:T(8,128)(2,1)} %param.14) | copy-start | bytes 344068
  10.9 120.1 %copy-start.6 = (f32[3584]{0:T(1024)S(1)}, f32[3584]{0:T(1024)}, u32[]{:S(2)}) copy-start(f32[3584]{0:T(1024)} %param.16) | copy-start | bytes 43012
  10.9 120.1 %copy-start.7 = (f32[3584]{0:T(1024)S(1)}, f32[3584]{0:T(1024)}, u32[]{:S(2)}) copy-start(f32[3584]{0:T(1024)} %param.15) | copy-start | bytes 43012
  10.9 260.8 %copy-start.2 = (s32[2,128,1024]{2,1,0:T(8,128)S(1)}, s32[2,128,1024]{2,1,0:T(8,128)}, u32[]{:S(2)}) copy-start(s32[2,128,1024]{2,1,0:T(8,128)} %param.18) | copy-start | bytes 3145732
  11.0 260.8 %copy-start.3 = (bf16[2,128,1024]{2,1,0:T(8,128)(2,1)S(1)}, bf16[2,128,1024]{2,1,0:T(8,128)(2,1)}, u32[]{:S(2)}) copy-start(bf16[2,128,1024]{2,1,0:T(8,128)(2,1)} %param.17) | copy-start | bytes 1572868
  11.0 118.5 %reduce-scatter.8.cloned.1.call-start = ((), (), s32[]{:S(2)}) async-start(), calls=%async_computation.4 | async-start | bytes 2293760 | tf_op jit(solution)/shard_map/reduce_scatter | solution.py:53
  98.9 700.2 %reduce-scatter.12.cloned.1.call-start = ((), (), s32[]{:S(2)}) async-start(), calls=%async_computation.7 | async-start | bytes 1146880
  130.9 637.3 %copy-start.9 = (bf16[2,32,16]{1,2,0:T(8,128)(2,1)S(1)}, bf16[2,32,16]{1,2,0:T(8,128)(2,1)}, u32[]{:S(2)}) copy-start(bf16[2,32,16]{1,2,0:T(8,128)(2,1)} %copy.21) | copy-start | bytes 6148
  768.3 1.7 copy-start.1
  769.9 525.3 %all-gather.6.cloned.1.call-start = ((), (), s32[]{:S(2)}) async-start(), calls=%async_computation.5 | async-start | bytes 2293760 | tf_op jit(solution)/shard_map/all_gather | solution.py:94
  1295.2 5.5 copy-start.8
Sparse Core Ops, SparseCore 0:
  11.2 81.4 all-gather.3
Sparse Core Ops, SparseCore 1:
  12.6 30.7 reduce-scatter.9
  99.0 30.5 reduce-scatter.7
  769.9 29.1 reduce-scatter.11
  802.0 36.1 all-gather.5
where the time goes:
time: 1310 us
  blocking collectives  1140 us (87%)
  waiting for transfers between devices  125 us (10%)
  matrix products  16.9 us (1%)
  between operations  15.9 us (1%)
    psum x1, blocking collectives, on_device(): lax.psum((down_local, up_share), ('dp', 'cand'))  495 us
    psum x1, blocking collectives, on_device(): summed_grad, loss_sum = lax.psum((score_vector, total), ('cand', 'tensor'))  493 us
    all_gather x1, blocking collectives, on_device(): all_scores = lax.all_gather(scores, ('cand', 'tensor'), axis=1, tiled=True)  140 us
    all_gather x1, waiting for transfers between devices, on_device(): full_weight = lax.all_gather(out_weight, 'cand', axis=0, tiled=True)  81.7 us
    reduce_scatter x1, waiting for transfers between devices, on_device(): lax.psum_scatter(head_terms.astype(jnp.bfloat16), 'tensor', scatter_dimen...  29 us
  transfers between devices with their start and end apart: 5, of which 3 were waited for; matrix products, arithmetic and copies ran while one was open for 1% of the time, Pallas kernels for 0%

commit v1 on v0

--- a/solution.py
+++ b/solution.py
@@ -111,7 +111,7 @@
     down_local = jnp.einsum(
         "qch,qcr->hr", context, full_adapter, preferred_element_type=jnp.float32
     )
-    down_grad, up_weight_gradient = lax.psum((down_local, up_share), ("dp", "cand"))
+    down_grad, up_weight_gradient = lax.psum(lax.psum((down_local, up_share), "cand"), "dp")
     return (context_grad, grad_rows, down_grad, up_weight_gradient, pair_loss)
 
 

time: 1310 us -> 959 us (0.73)
  the two profiles are of different devices: /device:TPU:16 before, /device:TPU:8 now
where the time goes in v1:
time: 959 us
  blocking collectives  739 us (77%)
  waiting for transfers between devices  175 us (18%)
  matrix products  16.9 us (2%)
  between operations  16 us (2%)
    psum x1, blocking collectives, on_device(): summed_grad, loss_sum = lax.psum((score_vector, total), ('cand', 'tensor'))  492 us
    all_gather x1, blocking collectives, on_device(): all_scores = lax.all_gather(scores, ('cand', 'tensor'), axis=1, tiled=True)  141 us
    psum x1, blocking collectives, on_device(): lax.psum((down_local, up_share), 'cand')  93.2 us
    all_gather x1, waiting for transfers between devices, on_device(): full_weight = lax.all_gather(out_weight, 'cand', axis=0, tiled=True)  81.7 us
    psum x1, waiting for transfers between devices, on_device(): lax.psum(lax.psum((down_local, up_share), 'cand'), 'dp')  48.9 us
    reduce_scatter x1, waiting for transfers between devices, on_device(): lax.psum_scatter(head_terms.astype(jnp.bfloat16), 'tensor', scatter_dimen...  29.4 us
  transfers between devices with their start and end apart: 6, of which 4 were waited for; matrix products, arithmetic and copies ran while one was open for 2% of the time, Pallas kernels for 0%

profile of v1, /device:TPU:8, one launch (start us, length us, event | category | flops | bytes accessed | tf_op | source)
XLA Modules:
  0.0 958.7 jit_solution(11741534377837041497)
XLA Ops:
  8.1 0.7 all-gather.4.cloned.1.call-update
  9.0 0.9 convolution_convert_fusion
  10.2 0.7 reshape.41
  11.0 81.7 %all-gather.4.cloned.1.call-done = bf16[3584,896]{1,0:T(8,128)(2,1)} async-done(((bf16[112,896]{1,0:T(8,128)(2,1)}), bf16[3584,896]{1,0:T(8,128)(2,1)}) %all-gather.4.cloned.1.call-update) | async-done | bytes 6422544 | tf_op jit(solution)/shard_map/all_gather | solution.py:49
  92.7 6.2 fusion.4
  99.0 0.8 reshape.42
  99.8 0.7 copy.21
  100.4 29.4 %reduce-scatter.8.cloned.1.call-done = bf16[2,32,3584]{2,1,0:T(8,128)(2,1)} async-done(((bf16[2,128,3584]{2,1,0:T(8,128)(2,1)}), bf16[2,32,3584]{2,1,0:T(8,128)(2,1)}) %reduce-scatter.8.cloned.1.call-update) | async-done | bytes 458768 | tf_op jit(solution)/shard_map/reduce_scatter | solution.py:53
  129.9 1.4 multiply_reduce_fusion.2
  131.6 140.7 %all-gather = f32[128,32,2]{1,2,0:T(2,128)S(1)} all-gather(f32[1,32,2]{1,2,0:T(2,128)S(1)} %bitcast.57), channel_id=1, replica_groups=mesh['dp'=4,'cand'=32,'tensor'=4] {'cand','tensor'}, dimensions={0}, use_global_device_ids=true | all-gather | bytes 33024 | tf_op jit(solution)/shard_map/all_gather | solution.py:70
  272.5 1.2 fusion.24
  274.0 491.7 %all-reduce = (f32[2,4096]{1,0:T(2,128)S(1)}, f32[2]{0:T(128)S(1)}, f32[2]{0:T(128)S(1)}) all-reduce(f32[2,4096]{1,0:T(2,128)S(1)} %sub.29, f32[2]{0:T(128)S(1)} %get-tuple-element.6, f32[2]{0:T(128)S(1)} %get-tuple-element.5), channel_id=1, replica_groups=mesh['dp'=4,'cand'=32,'tensor'=4] {'cand','tensor'}, use_global_device_ids=true, to_apply=%region_6.7 | all-reduce | flops 8196 | bytes 65568 | tf_op jit(solution)/shard_map/psum | solution.py:78
  765.7 1.2 fusion.32
  767.8 1.3 copy.22
  769.9 1.4 fusion.13
  771.5 13.4 %all_gather.15 = bf16[2,128,16]{2,0,1:T(2,128)(2,1)S(1)} all-gather(bf16[2,32,16]{2,0,1:T(2,128)(2,1)S(1)} %copy.17), channel_id=1, replica_groups=mesh['dp'=4,'cand'=32,'tensor'=4] {'tensor'}, dimensions={1}, use_global_device_ids=true | all-gather | bytes 10240 | tf_op jit(solution)/shard_map/all_gather | solution.py:95
  785.1 13.3 %reduce-scatter.12.cloned.1.call-done = bf16[896,16]{1,0:T(8,128)(2,1)} async-done(((bf16[3584,16]{1,0:T(8,128)(2,1)}), bf16[896,16]{1,0:T(8,128)(2,1)}) %reduce-scatter.12.cloned.1.call-update) | async-done | bytes 28688
  798.4 1.0 copy.23
  799.4 93.2 %all-reduce.7 = (f32[896,16]{0,1:T(8,128)}, f32[16,896]{1,0:T(8,128)}) all-reduce(f32[896,16]{0,1:T(8,128)S(1)} %convolution_bitcast_fusion.1, bf16[16,896]{1,0:T(8,128)(2,1)S(1)} %copy.23), channel_id=1, replica_groups=mesh['dp'=4,'cand'=32,'tensor'=4] {'cand'}, use_global_device_ids=true, to_apply=%region_10.11 | all-reduce | flops 28672 | bytes 200704 | tf_op jit(solution)/shard_map/psum | solution.py:114
  892.7 5.5 fusion
  898.2 1.1 fusion.12
  899.3 48.9 %all-reduce.6.cloned.1.call-done = (f32[896,16]{0,1:T(8,128)}, f32[16,896]{1,0:T(8,128)}) async-done(((f32[896,16]{0,1:T(8,128)}, f32[16,896]{1,0:T(8,128)}), (f32[896,16]{0,1:T(8,128)}, f32[16,896]{1,0:T(8,128)})) %all-reduce.6.cloned.1.call-update) | async-done | bytes 114704 | tf_op jit(solution)/shard_map/psum | solution.py:114
  948.2 1.4 copy.31
  949.6 1.4 copy.32
  (54 shorter events, 3.5 us)
Async XLA Ops:
  8.0 1.0 copy-start
  8.0 84.7 %all-gather.4.cloned.1.call-start = ((), (), s32[]{:S(2)}) async-start(), calls=%async_computation.3 | async-start | bytes 6623232 | tf_op jit(solution)/shard_map/all_gather | solution.py:49
  8.7 90.2 %reduce-scatter.10.cloned.1.call-start = ((), (), s32[]{:S(2)}) async-start(), calls=%async_computation.6 | async-start | bytes 40960
  10.9 119.0 %copy-start.4 = (bf16[2,32,3584]{2,1,0:T(8,128)(2,1)S(1)}, bf16[2,32,3584]{2,1,0:T(8,128)(2,1)}, u32[]{:S(2)}) copy-start(bf16[2,32,3584]{2,1,0:T(8,128)(2,1)} %param.11) | copy-start | bytes 1376260
  10.9 119.0 %copy-start.5 = (bf16[16,3584]{1,0:T(8,128)(2,1)S(1)}, bf16[16,3584]{1,0:T(8,128)(2,1)}, u32[]{:S(2)}) copy-start(bf16[16,3584]{1,0:T(8,128)(2,1)} %param.14) | copy-start | bytes 344068
  10.9 120.4 %copy-start.6 = (f32[3584]{0:T(1024)S(1)}, f32[3584]{0:T(1024)}, u32[]{:S(2)}) copy-start(f32[3584]{0:T(1024)} %param.16) | copy-start | bytes 43012
  10.9 120.4 %copy-start.7 = (f32[3584]{0:T(1024)S(1)}, f32[3584]{0:T(1024)}, u32[]{:S(2)}) copy-start(f32[3584]{0:T(1024)} %param.15) | copy-start | bytes 43012
  10.9 261.6 %copy-start.2 = (s32[2,128,1024]{2,1,0:T(8,128)S(1)}, s32[2,128,1024]{2,1,0:T(8,128)}, u32[]{:S(2)}) copy-start(s32[2,128,1024]{2,1,0:T(8,128)} %param.18) | copy-start | bytes 3145732
  11.0 261.6 %copy-start.3 = (bf16[2,128,1024]{2,1,0:T(8,128)(2,1)S(1)}, bf16[2,128,1024]{2,1,0:T(8,128)(2,1)}, u32[]{:S(2)}) copy-start(bf16[2,128,1024]{2,1,0:T(8,128)(2,1)} %param.17) | copy-start | bytes 1572868
  11.0 118.9 %reduce-scatter.8.cloned.1.call-start = ((), (), s32[]{:S(2)}) async-start(), calls=%async_computation.4 | async-start | bytes 2293760 | tf_op jit(solution)/shard_map/reduce_scatter | solution.py:53
  98.9 699.5 %reduce-scatter.12.cloned.1.call-start = ((), (), s32[]{:S(2)}) async-start(), calls=%async_computation.7 | async-start | bytes 1146880
  131.3 636.3 %copy-start.9 = (bf16[2,32,16]{1,2,0:T(8,128)(2,1)S(1)}, bf16[2,32,16]{1,2,0:T(8,128)(2,1)}, u32[]{:S(2)}) copy-start(bf16[2,32,16]{1,2,0:T(8,128)(2,1)} %copy.21) | copy-start | bytes 6148
  767.6 1.7 copy-start.1
  769.2 123.6 %all-gather.6.cloned.1.call-start = ((), (), s32[]{:S(2)}) async-start(), calls=%async_computation.5 | async-start | bytes 2293760 | tf_op jit(solution)/shard_map/all_gather | solution.py:94
  769.9 178.3 %all-reduce.6.cloned.1.call-start = ((), (), s32[]{:S(2)}) async-start(), calls=%async_computation.8 | async-start | bytes 229376 | tf_op jit(solution)/shard_map/psum | solution.py:114
  892.7 5.5 copy-start.8
Sparse Core Ops, SparseCore 0:
  11.2 81.4 all-gather.3
Sparse Core Ops, SparseCore 1:
  12.6 31.1 reduce-scatter.9
  99.0 30.8 reduce-scatter.7
  769.2 29.1 reduce-scatter.11
  801.3 37.2 all-gather.5
  892.8 55.4 all-reduce.5
